TPU v7x, 32 devices: a whole 2x2x4 slice. The times are simulated.
32 devices in a mesh: row: 4 (over y, x), col: 8 (over z, core).
Axes of the slice: x: 2, y: 2, z: 4, core: 2. Of those that a mesh axis runs over, the one named last changes fastest.
Arguments:
- trailing_slab: bfloat16 [24576, 8192], P('row', 'col'), may hold values from -6 to 6
- panel_cols: bfloat16 [24576, 512], P('row', 'col'), may hold values from -0.25 to 0.25
- head_slab: bfloat16 [512, 8192], P('row', 'col'), may hold values from -6 to 6
- coupling: bfloat16 [2, 256, 256], replicated, may hold values from -0.25 to 0.25
- lower_inverses: bfloat16 [2, 256, 256], replicated, may hold values from -1.5 to 1.5, as said below
- upper_inverses: bfloat16 [2, 256, 256], replicated, may hold values from -1.5 to 1.5, as said below
Outputs:
- trailing: bfloat16 [24576, 8192], P('row', 'col')
Inputs may be any that keep to these rules, and one draw needn't show every extreme that they name: `lower_inverses`: each of the two [256, 256] blocks is lower triangular with unit diagonal. `upper_inverses`: each of the two [256, 256] blocks is upper triangular with diagonal between 0.5 and 1.5.
All inputs are finite; a program needn't handle non-finite values.
Results may differ from a plain program's by a relative error of at most 0.0067.
Values may be sent and summed in bfloat16 or wider, within the bound.
No kernel may reach another device: no remote copies, remote signals or barrier semaphores. Data moves between devices by JAX's collectives and lax.ppermute only.
A program may use at most 128 MiB of HBM per device.

v0:
```python
import jax
import jax.numpy as jnp
from jax import lax
from jax.sharding import PartitionSpec as P


def product(left, right):
    return jnp.dot(left, right, preferred_element_type=jnp.float32)


def factor_panel(panel_block, upper_mid, upper_inverses):
    width = upper_mid.shape[0]
    lower_first = product(panel_block[:, :width], upper_inverses[0]).astype(jnp.bfloat16)
    panel_second = (
        panel_block[:, width:].astype(jnp.float32) - product(lower_first, upper_mid)
    ).astype(jnp.bfloat16)
    lower_second = product(panel_second, upper_inverses[1]).astype(jnp.bfloat16)
    return jnp.concatenate([lower_first, lower_second], axis=1)


def apply_update(slab_part, lower_block, upper_both):
    result = slab_part.astype(jnp.float32) - product(lower_block, upper_both)
    return result.astype(jnp.bfloat16)


def on_device(trailing_slab, panel_cols, head_slab, coupling, lower_inverses, upper_inverses):
    width = coupling.shape[1]
    head_full = lax.all_gather(head_slab, "row", axis=0, tiled=True)
    upper_mid = product(lower_inverses[0], coupling[0]).astype(jnp.bfloat16)
    upper_first = product(lower_inverses[0], head_full[:width]).astype(jnp.bfloat16)
    lower_head = product(coupling[1], upper_inverses[0]).astype(jnp.bfloat16)
    head_second = (head_full[width:].astype(jnp.float32) - product(lower_head, upper_first)).astype(
        jnp.bfloat16
    )
    upper_second = product(lower_inverses[1], head_second).astype(jnp.bfloat16)
    upper_both = jnp.concatenate([upper_first, upper_second], axis=0)
    panel_full = lax.all_gather(panel_cols, "col", axis=1, tiled=True)
    lower_block = factor_panel(panel_full, upper_mid, upper_inverses)
    return apply_update(trailing_slab, lower_block, upper_both)


def solution(mesh):
    in_specs = (P("row", "col"), P("row", "col"), P("row", "col"), P(), P(), P())
    out_specs = P("row", "col")
    return jax.shard_map(
        on_device, mesh=mesh, in_specs=in_specs, out_specs=out_specs, check_vma=False
    )
```

profile of v0, /device:TPU:0, one launch (start us, length us, event | category | flops | bytes accessed | tf_op | source)
XLA Modules:
  0.0 133.2 jit_solution(17150895435019928692)
XLA Ops:
  6.5 0.0 all-gather.5.cloned.1.call-start
  6.5 0.7 all-gather.5.cloned.1.call-update
  7.3 0.0 all-gather.3.cloned.1.call-start
  7.3 0.7 all-gather.3.cloned.1.call-update
  8.0 1.2 convolution_convert_fusion.4
  9.2 1.2 convolution_convert_fusion.5
  10.3 0.0 copy-start.1
  10.3 28.1 %all-gather.5.cloned.1.call-done = bf16[512,1024]{1,0:T(8,128)(2,1)} async-done(((bf16[128,1024]{1,0:T(8,128)(2,1)}), bf16[512,1024]{1,0:T(8,128)(2,1)}) %all-gather.5.cloned.1.call-update) | async-done | bytes 1048592 | tf_op jit(solution)/shard_map/all_gather | solution.py:28
  38.4 1.4 %convolution_convert_fusion.3 = bf16[256,1024]{1,0:T(8,128)(2,1)S(1)} fusion(bf16[512,1024]{1,0:T(8,128)(2,1)} %all-gather.5.cloned.1.call-done, bf16[2,256,256]{2,1,0:T(8,128)(2,1)} %param.10), kind=kOutput, calls=%fused_computation.11 | convolution fusion | flops 134479872 | bytes 1179648 | tf_op jit(solution)/shard_map/dot_general | solution.py:8
  39.9 0.0 copy-start
  39.9 2.6 %fusion.6 = bf16[256,1024]{1,0:T(8,128)(2,1)} fusion(bf16[256,256]{1,0:T(8,128)(2,1)S(1)} %convolution_convert_fusion.4, bf16[256,1024]{1,0:T(8,128)(2,1)S(1)} %convolution_convert_fusion.3, bf16[512,1024]{1,0:T(8,128)(2,1)} %all-gather.5.cloned.1.call-done, bf16[2,256,256]{2,1,0:T(8,128)(2,1)} %param.10), kind=kOutput, calls=%fused_computation.13 | convolution fusion | flops 269484032 | bytes 1835008 | tf_op jit(solution)/shard_map/dot_general | solution.py:8
  42.5 0.0 copy-done
  42.5 62.3 %all-gather.3.cloned.1.call-done = bf16[6144,512]{0,1:T(8,128)(2,1)} async-done(((bf16[6144,64]{0,1:T(8,128)(2,1)}), bf16[6144,512]{0,1:T(8,128)(2,1)}) %all-gather.3.cloned.1.call-update) | async-done | bytes 6291472 | tf_op jit(solution)/shard_map/all_gather | solution.py:37
  104.8 2.9 %convolution_convert_fusion.1 = bf16[6144,256]{0,1:T(8,128)(2,1)S(1)} fusion(bf16[6144,512]{0,1:T(8,128)(2,1)} %all-gather.3.cloned.1.call-done, bf16[2,256,256]{2,1,0:T(8,128)(2,1)} %param.11), kind=kOutput, calls=%fused_computation.4 | convolution fusion | flops 806879232 | bytes 6422528 | tf_op jit(solution)/shard_map/dot_general | solution.py:8
  107.7 0.0 copy-done.1
  107.7 5.5 %convolution_convert_fusion = bf16[6144,256]{0,1:T(8,128)(2,1)} fusion(bf16[6144,256]{0,1:T(8,128)(2,1)S(1)} %convolution_convert_fusion.1, bf16[256,256]{1,0:T(8,128)(2,1)S(1)} %convolution_convert_fusion.5, bf16[6144,512]{0,1:T(8,128)(2,1)} %all-gather.3.cloned.1.call-done, bf16[2,256,256]{2,1,0:T(8,128)(2,1)S(1)} %copy-done.1), kind=kOutput, calls=%fused_computation.3 | convolution fusion | flops 1616904192 | bytes 9699328 | tf_op jit(solution)/shard_map/dot_general | solution.py:8
  113.2 13.2 %subtract_convert_fusion = bf16[6144,1024]{1,0:T(8,128)(2,1)} fusion(bf16[6144,1024]{1,0:T(8,128)(2,1)} %param.6, bf16[6144,256]{0,1:T(8,128)(2,1)} %convolution_convert_fusion, bf16[6144,256]{0,1:T(8,128)(2,1)S(1)} %convolution_convert_fusion.1, bf16[256,1024]{1,0:T(8,128)(2,1)} %fusion.6, bf16[256,1024]{1,0:T(8,128)(2,1)} %copy-done), kind=kOutput, calls=%fused_computation | convolution fusion | flops 6476005376 | bytes 32505856 | tf_op jit(solution)/shard_map/dot_general | solution.py:8
Async XLA Ops:
  6.5 31.9 %all-gather.5.cloned.1.call-start = ((), (), s32[]{:S(2)}) async-start(), calls=%async_computation.1 | async-start | bytes 1310720 | tf_op jit(solution)/shard_map/all_gather | solution.py:28
  7.3 97.5 %all-gather.3.cloned.1.call-start = ((), (), s32[]{:S(2)}) async-start(), calls=%async_computation | async-start | bytes 7077888 | tf_op jit(solution)/shard_map/all_gather | solution.py:37
  10.3 97.4 %copy-start.1 = (bf16[2,256,256]{2,1,0:T(8,128)(2,1)S(1)}, bf16[2,256,256]{2,1,0:T(8,128)(2,1)}, u32[]{:S(2)}) copy-start(bf16[2,256,256]{2,1,0:T(8,128)(2,1)} %param.11) | copy-start | bytes 786436
  39.9 2.6 %copy-start = (bf16[256,1024]{1,0:T(8,128)(2,1)}, bf16[256,1024]{1,0:T(8,128)(2,1)S(1)}, u32[]{:S(2)}) copy-start(bf16[256,1024]{1,0:T(8,128)(2,1)S(1)} %convolution_convert_fusion.3) | copy-start | bytes 1572868
Sparse Core Ops, SparseCore 0:
  9.2 29.2 all-gather.4
  40.1 64.6 all-gather.2
where the time goes:
time: 133 us
  waiting for transfers between devices  91.8 us (69%)
  matrix products  27.9 us (21%)
  between operations  13.5 us (10%)
    all_gather x1, waiting for transfers between devices, on_device(): panel_full = lax.all_gather(panel_cols, 'col', axis=1, tiled=True)  62.3 us
    all_gather x1, waiting for transfers between devices, on_device(): head_full = lax.all_gather(head_slab, 'row', axis=0, tiled=True)  28.1 us
    dot_general x7, matrix products, product(): return jnp.dot(left, right, preferred_element_type=jnp.float32)  27.9 us
  transfers between devices with their start and end apart: 2, of which 2 were waited for; matrix products, arithmetic and copies ran while one was open for 5% of the time, Pallas kernels for 0%

commit v1 on v0

--- a/solution.py
+++ b/solution.py
@@ -2,6 +2,27 @@
 import jax.numpy as jnp
 from jax import lax
 from jax.sharding import PartitionSpec as P
+
+
+def joined_along(blocks, dim):
+    blocks = jnp.moveaxis(blocks, 0, dim)
+    shape = blocks.shape
+    return blocks.reshape(*shape[:dim], shape[dim] * shape[dim + 1], *shape[dim + 2 :])
+
+
+def grow_blocks(x, axis):
+    length, position = (lax.axis_size(axis), lax.axis_index(axis))
+    blocks, stride = (x[None], 1)
+    while stride < length:
+        other = lax.ppermute(blocks, axis, [(i, i ^ stride) for i in range(length)])
+        low = position & stride == 0
+        blocks = jnp.concatenate([jnp.where(low, blocks, other), jnp.where(low, other, blocks)])
+        stride *= 2
+    return blocks
+
+
+def doubled_up(value, axis, dim):
+    return joined_along(grow_blocks(value, axis), dim)
 
 
 def product(left, right):
@@ -25,7 +46,7 @@
 
 def on_device(trailing_slab, panel_cols, head_slab, coupling, lower_inverses, upper_inverses):
     width = coupling.shape[1]
-    head_full = lax.all_gather(head_slab, "row", axis=0, tiled=True)
+    head_full = doubled_up(head_slab, "row", 0)
     upper_mid = product(lower_inverses[0], coupling[0]).astype(jnp.bfloat16)
     upper_first = product(lower_inverses[0], head_full[:width]).astype(jnp.bfloat16)
     lower_head = product(coupling[1], upper_inverses[0]).astype(jnp.bfloat16)

time: 133 us -> 105 us (0.79)
  waiting for transfers between devices: 91.8 us -> 59.9 us
  starting transfers between devices: 0.04 us -> 4.87 us
  matrix products: 27.9 us -> 25.5 us
    all_gather x1 -> x0, waiting for transfers between devices: 28.1 us -> none  [on_device(): head_full = lax.all_gather(head_slab, 'row', axis=0, tiled=True)]
    all_gather x1, waiting for transfers between devices: 62.3 us -> 42.5 us  [on_device(): panel_full = lax.all_gather(panel_cols, 'col', axis=1, tiled=True)]
    ppermute x0 -> x2, waiting for transfers between devices: none -> 16.7 us  [grow_blocks(): other = lax.ppermute(blocks, axis, [(i, i ^ stride) for i in range(length)])]
    ppermute x0 -> x2, starting transfers between devices: none -> 4.87 us  [grow_blocks(): other = lax.ppermute(blocks, axis, [(i, i ^ stride) for i in range(length)])]
    dot_general x7, matrix products: 27.9 us -> 25.5 us  [product(): return jnp.dot(left, right, preferred_element_type=jnp.float32)]
  transfers between devices with their start and end apart: 2 -> 3, of which waited for: 2 -> 3; matrix products, arithmetic and copies ran while one was open for 5% -> 5% of each run, Pallas kernels for 0% -> 0%
where the time goes in v1:
time: 105 us
  waiting for transfers between devices  59.9 us (57%)
  matrix products  25.5 us (24%)
  between operations  13.5 us (13%)
  starting transfers between devices  4.87 us (5%)
  other arithmetic  1.11 us (1%)
    all_gather x1, waiting for transfers between devices, on_device(): panel_full = lax.all_gather(panel_cols, 'col', axis=1, tiled=True)  42.5 us
    dot_general x7, matrix products, product(): return jnp.dot(left, right, preferred_element_type=jnp.float32)  25.5 us
    ppermute x2, waiting for transfers between devices, grow_blocks(): other = lax.ppermute(blocks, axis, [(i, i ^ stride) for i in range(length)])  16.7 us
    ppermute x2, starting transfers between devices, grow_blocks(): other = lax.ppermute(blocks, axis, [(i, i ^ stride) for i in range(length)])  4.87 us
  transfers between devices with their start and end apart: 3, of which 3 were waited for; matrix products, arithmetic and copies ran while one was open for 5% of the time, Pallas kernels for 0%

profile of v1, /device:TPU:0, one launch (start us, length us, event | category | flops | bytes accessed | tf_op | source)
XLA Modules:
  0.0 104.9 jit_solution(8720201910342270022)
XLA Ops:
  6.5 0.0 copy-start.1
  6.5 0.0 copy-start.3
  6.5 0.0 all-gather.2.cloned.1.call-start
  6.5 0.7 all-gather.2.cloned.1.call-update
  7.3 3.0 %collective-permute-start = (bf16[1,128,1024]{2,1,0:T(8,128)(2,1)}, bf16[1,128,1024]{2,1,0:T(8,128)(2,1)S(1)}, u32[]{:S(2)}, u32[]{:S(2)}) collective-permute-start(bf16[1,128,1024]{2,1,0:T(8,128)(2,1)} %bitcast.40), channel_id=1, source_target_pairs={{0,8},{8,0},{16,24},{24,16},{1,9},{9,1},{17,25},{25,17},{2,10},{10... | collective-permute-start | bytes 786440 | tf_op jit(solution)/shard_map/ppermute | solution.py:17
  10.3 6.5 %collective-permute-done = bf16[1,128,1024]{2,1,0:T(8,128)(2,1)S(1)} collective-permute-done((bf16[1,128,1024]{2,1,0:T(8,128)(2,1)}, bf16[1,128,1024]{2,1,0:T(8,128)(2,1)S(1)}, u32[]{:S(2)}, u32[]{:S(2)}) %collective-permute-start) | collective-permute-done | bytes 262176 | tf_op jit(solution)/shard_map/ppermute | solution.py:17
  16.8 1.0 broadcast_select_fusion.3
  17.8 0.1 pad_maximum_fusion
  17.9 1.8 %collective-permute-start.1 = (bf16[2,128,1024]{2,1,0:T(8,128)(2,1)S(1)}, bf16[2,128,1024]{2,1,0:T(8,128)(2,1)S(1)}, u32[]{:S(2)}, u32[]{:S(2)}) collective-permute-start(bf16[2,128,1024]{2,1,0:T(8,128)(2,1)S(1)} %pad_maximum_fusion), channel_id=1, source_target_pairs={{0,16},{8,24},{16,0},{24,8},{1,17},{9,25},{17,1},{25,9},{2,18},{10... | collective-permute-start | bytes 1572872 | tf_op jit(solution)/shard_map/ppermute | solution.py:17
  19.7 1.2 %convolution_convert_fusion.5 = bf16[256,256]{1,0:T(8,128)(2,1)S(1)} fusion(bf16[2,256,256]{2,1,0:T(8,128)(2,1)} %param.9, bf16[2,256,256]{2,1,0:T(8,128)(2,1)} %param.10), kind=kOutput, calls=%fused_computation.13 | convolution fusion | flops 33619968 | bytes 393216 | tf_op jit(solution)/shard_map/dot_general | solution.py:29
  20.9 10.2 %collective-permute-done.1 = bf16[2,128,1024]{2,1,0:T(8,128)(2,1)S(1)} collective-permute-done((bf16[2,128,1024]{2,1,0:T(8,128)(2,1)S(1)}, bf16[2,128,1024]{2,1,0:T(8,128)(2,1)S(1)}, u32[]{:S(2)}, u32[]{:S(2)}) %collective-permute-start.1) | collective-permute-done | bytes 524320 | tf_op jit(solution)/shard_map/ppermute | solution.py:17
  31.0 0.1 broadcast_select_fusion
  31.1 1.2 %convolution_convert_fusion.3 = bf16[1024,256]{0,1:T(8,128)(2,1)S(1)} fusion(bf16[256,1024]{1,0:T(8,128)(2,1)S(1)} %bitcast.39, bf16[2,256,256]{2,1,0:T(8,128)(2,1)} %param.10), kind=kOutput, calls=%fused_computation.10 | convolution fusion | flops 134479872 | bytes 1179648 | tf_op jit(solution)/shard_map/dot_general | solution.py:29
  32.3 0.0 copy-done.3
  32.3 0.0 copy-done.2
  32.3 0.0 copy-start
  32.3 0.4 fusion.6
  32.8 0.0 copy-done.1
  32.8 1.1 %fusion.5 = bf16[256,1024]{1,0:T(8,128)(2,1)} fusion(f32[256,1024]{1,0:T(8,128)S(1)} %fusion.6, bf16[256,1024]{1,0:T(8,128)(2,1)S(1)} %bitcast.37, bf16[2,256,256]{2,1,0:T(8,128)(2,1)S(1)} %copy-done.1), kind=kOutput, calls=%fused_computation.11 | convolution fusion | flops 135266304 | bytes 2228224 | tf_op jit(solution)/shard_map/dot_general | solution.py:29
  33.9 0.0 copy-done
  33.9 42.5 %all-gather.2.cloned.1.call-done = bf16[6144,512]{0,1:T(8,128)(2,1)} async-done(((bf16[6144,64]{0,1:T(8,128)(2,1)}), bf16[6144,512]{0,1:T(8,128)(2,1)}) %all-gather.2.cloned.1.call-update) | async-done | bytes 6291472 | tf_op jit(solution)/shard_map/all_gather | solution.py:58
  76.4 2.9 %convolution_convert_fusion.1 = bf16[6144,256]{0,1:T(8,128)(2,1)S(1)} fusion(bf16[6144,512]{0,1:T(8,128)(2,1)} %all-gather.2.cloned.1.call-done, bf16[2,256,256]{2,1,0:T(8,128)(2,1)} %param.11), kind=kOutput, calls=%fused_computation.4 | convolution fusion | flops 806879232 | bytes 6422528 | tf_op jit(solution)/shard_map/dot_general | solution.py:29
  79.3 5.5 %convolution_convert_fusion = bf16[6144,256]{0,1:T(8,128)(2,1)} fusion(bf16[6144,256]{0,1:T(8,128)(2,1)S(1)} %convolution_convert_fusion.1, bf16[256,256]{1,0:T(8,128)(2,1)S(1)} %convolution_convert_fusion.5, bf16[6144,512]{0,1:T(8,128)(2,1)} %all-gather.2.cloned.1.call-done, bf16[2,256,256]{2,1,0:T(8,128)(2,1)} %param.11), kind=kOutput, calls=%fused_computation.3 | convolution fusion | flops 1616904192 | bytes 9699328 | tf_op jit(solution)/shard_map/dot_general | solution.py:29
  84.8 13.2 %subtract_convert_fusion = bf16[6144,1024]{1,0:T(8,128)(2,1)} fusion(bf16[6144,1024]{1,0:T(8,128)(2,1)} %param.6, bf16[6144,256]{0,1:T(8,128)(2,1)} %convolution_convert_fusion, bf16[6144,256]{0,1:T(8,128)(2,1)S(1)} %convolution_convert_fusion.1, bf16[256,1024]{1,0:T(8,128)(2,1)} %fusion.5, bf16[256,1024]{1,0:T(8,128)(2,1)} %bitcast.38), kind=kOutput, calls=%fused_computation | convolution fusion | flops 6476005376 | bytes 32505856 | tf_op jit(solution)/shard_map/dot_general | solution.py:29
  (1 shorter events, 0.0 us)
Async XLA Ops:
  6.5 26.2 %copy-start.1 = (bf16[2,256,256]{2,1,0:T(8,128)(2,1)S(1)}, bf16[2,256,256]{2,1,0:T(8,128)(2,1)}, u32[]{:S(2)}) copy-start(bf16[2,256,256]{2,1,0:T(8,128)(2,1)} %param.10) | copy-start | bytes 786436
  6.5 25.8 %copy-start.3 = (bf16[2,256,256]{2,1,0:T(8,128)(2,1)S(1)}, bf16[2,256,256]{2,1,0:T(8,128)(2,1)}, u32[]{:S(2)}) copy-start(bf16[2,256,256]{2,1,0:T(8,128)(2,1)} %param.9) | copy-start | bytes 786436
  6.5 25.8 %copy-start.2 = (bf16[2,256,256]{2,1,0:T(8,128)(2,1)S(1)}, bf16[2,256,256]{2,1,0:T(8,128)(2,1)}, u32[]{:S(2)}) copy-start(bf16[2,256,256]{2,1,0:T(8,128)(2,1)} %param.11) | copy-start | bytes 786436
  6.5 69.9 %all-gather.2.cloned.1.call-start = ((), (), s32[]{:S(2)}) async-start(), calls=%async_computation | async-start | bytes 7077888 | tf_op jit(solution)/shard_map/all_gather | solution.py:58
  7.3 9.5 %collective-permute-start = (bf16[1,128,1024]{2,1,0:T(8,128)(2,1)}, bf16[1,128,1024]{2,1,0:T(8,128)(2,1)S(1)}, u32[]{:S(2)}, u32[]{:S(2)}) collective-permute-start(bf16[1,128,1024]{2,1,0:T(8,128)(2,1)} %bitcast.40), channel_id=1, source_target_pairs={{0,8},{8,0},{16,24},{24,16},{1,9},{9,1},{17,25},{25,17},{2,10},{10... | collective-permute-start | bytes 786440 | tf_op jit(solution)/shard_map/ppermute | solution.py:17
  17.9 13.2 %collective-permute-start.1 = (bf16[2,128,1024]{2,1,0:T(8,128)(2,1)S(1)}, bf16[2,128,1024]{2,1,0:T(8,128)(2,1)S(1)}, u32[]{:S(2)}, u32[]{:S(2)}) collective-permute-start(bf16[2,128,1024]{2,1,0:T(8,128)(2,1)S(1)} %pad_maximum_fusion), channel_id=1, source_target_pairs={{0,16},{8,24},{16,0},{24,8},{1,17},{9,25},{17,1},{25,9},{2,18},{10... | collective-permute-start | bytes 1572872 | tf_op jit(solution)/shard_map/ppermute | solution.py:17
  32.3 1.6 %copy-start = (bf16[1024,256]{0,1:T(8,128)(2,1)}, bf16[1024,256]{0,1:T(8,128)(2,1)S(1)}, u32[]{:S(2)}) copy-start(bf16[1024,256]{0,1:T(8,128)(2,1)S(1)} %convolution_convert_fusion.3) | copy-start | bytes 1572868
Sparse Core Ops, SparseCore 0:
  9.0 67.4 all-gather.1
